TPU v7x, 256 devices: a whole 4x4x8 slice. The times are simulated.
256 devices in a mesh: rep: 4 (over x_hi, core), tp: 32 (over z, y), dec: 2 (over x_lo).
Axes of the slice: x: 4 (x_hi: 2, x_lo: 2; x = x_hi * 2 + x_lo), y: 4, z: 8, core: 2. Of those that a mesh axis runs over, the one named last changes fastest.
Arguments:
- residual: bfloat16 [4096, 4096], P(('rep', 'tp', 'dec')), may hold values from -6 to 6
- queries: bfloat16 [128, 2, 16, 4096], P('rep', 'dec', None, 'tp'), may hold values from -64 to 64
- kv_pool: bfloat16 [256, 8, 128, 256], P(('rep', 'tp', 'dec')), may hold values from -8 to 8
- prior_len: int32 [16], P('rep'), may hold values from 0 to 1792, as said below
- page_table: int32 [16, 16], P('rep'), may hold values from -1 to 255, as said below
- page_target: int32 [256], P(('rep', 'tp', 'dec')), may hold values from 0 to 3, as said below
- out_weight: bfloat16 [4096, 4096], P('tp'), may hold values from -0.5 to 0.5
- moe_gain: float32 [4096], replicated, may hold values from 0.1 to 1.9
- expert_ids: int32 [4096, 2], P(('rep', 'tp', 'dec')), may hold values from 0 to 7, as said below
- expert_gates: float32 [4096, 2], P(('rep', 'tp', 'dec')), may hold values from 0.1 to 1
- w_gate: bfloat16 [2, 14336, 4096], P('dec', 'tp'), may hold values from -0.09375 to 0.09375
- w_up: bfloat16 [2, 14336, 4096], P('dec', 'tp'), may hold values from -0.09375 to 0.09375
- w_down: bfloat16 [2, 14336, 4096], P('dec', 'tp'), may hold values from -0.1875 to 0.1875
Outputs:
- layer_out: bfloat16 [4096, 4096], P(('rep', 'tp', 'dec'))
- decode_pages: bfloat16 [256, 8, 128, 256], P(('rep', 'tp', 'dec'))
Inputs may be any that keep to these rules, and one draw needn't show every extreme that they name: `prior_len`: each value is a multiple of 256; in every rep index's 4 requests one request has the largest value. `page_table`: for request q, the first (prior_len[q] + 256) // 128 entries are distinct slots among the 64 slots of q's rep index (slots r * 64 to r * 64 + 63), no slot named twice in a rep index; the other entries are -1. Slots that no entry names hold data that attention never reads. `page_target`: for every m, the slots r * 64 + m over all rep indices r go to distinct rep indices. `expert_ids`: each row names two different experts; among the 16 rows of each device (aligned blocks of rows) every expert is named by exactly 4 rows.
All inputs are finite; a program needn't handle non-finite values.
Results may differ from a plain program's by a relative error of at most 0.02.
Values may be sent and summed in bfloat16 or wider, within the bound.
A program may use at most 64 MiB of HBM per device.

v0:
```python
import jax
import jax.numpy as jnp
from jax import lax
from jax.sharding import PartitionSpec as P

QH = 32
KVH = 8
EXPERTS = 8
TOPK = 2
EXP_WIN = 2


def hand_over(kv_pool, page_target):
    rep_size = lax.axis_size("rep")
    owners = jnp.arange(rep_size, dtype=jnp.int32)
    selected = (page_target[None, :] == owners[:, None])[:, :, None, None, None]
    outgoing = jnp.where(selected, kv_pool[None], jnp.zeros((), kv_pool.dtype))
    incoming = lax.all_to_all(outgoing, "rep", split_axis=0, concat_axis=0, tiled=True)
    return jnp.sum(incoming, axis=0)


def on_device(
    residual,
    queries,
    kv_pool,
    prior_len,
    page_table,
    page_target,
    out_weight,
    moe_gain,
    expert_ids,
    expert_gates,
    w_gate,
    w_up,
    w_down,
):
    tp_size = lax.axis_size("tp")
    dec_size = lax.axis_size("dec")
    dec_index = lax.axis_index("dec")
    slots_dev, kv_heads, page_rows, both_dim = kv_pool.shape
    head_dim = both_dim // 2
    heads_dev = queries.shape[3] // head_dim
    group_size = QH // KVH
    kv_dev = max(1, heads_dev // group_size)
    copies = max(1, group_size // heads_dev)
    per_kv = heads_dev // kv_dev
    requests = prior_len.shape[0]
    tok_dev = queries.shape[2]
    half_rows = queries.shape[0] * tok_dev // requests
    pages_max = page_table.shape[1]
    team_size = tp_size * dec_size
    spread = jnp.repeat(kv_pool, copies, axis=1).reshape(
        slots_dev, tp_size, kv_dev, page_rows, both_dim
    )
    holder = page_table // slots_dev % team_size
    number = page_table % slots_dev
    outgoing = jnp.broadcast_to(
        spread[:, :, None], (slots_dev, tp_size, dec_size, kv_dev, page_rows, both_dim)
    )
    outgoing = outgoing.reshape(slots_dev, team_size, kv_dev, page_rows, both_dim)
    received = lax.all_to_all(outgoing, ("tp", "dec"), split_axis=1, concat_axis=0, tiled=True)
    local_index = holder * slots_dev + number
    received = received.reshape(team_size * slots_dev, kv_dev, page_rows, both_dim)
    gathered_pages = received[local_index]
    keys_part = gathered_pages[..., :head_dim]
    values_part = gathered_pages[..., head_dim:]
    query_rows = queries.reshape(requests, half_rows, kv_dev, per_kv, head_dim)
    key_count = pages_max * page_rows
    scores = jnp.einsum(
        "rukgd,rpkwd->rukgpw", query_rows, keys_part, preferred_element_type=jnp.float32
    )
    scores = scores.reshape(requests, half_rows, kv_dev, per_kv, key_count) * head_dim ** (-0.5)
    position = jnp.arange(key_count, dtype=jnp.int32)
    local_row = jnp.arange(half_rows, dtype=jnp.int32)
    offset = (local_row // tok_dev * dec_size + dec_index) * tok_dev + local_row % tok_dev
    last_seen = prior_len[:, None] + offset[None, :]
    visible = (position[None, None, :] <= last_seen[:, :, None])[:, :, None, None, :]
    scores = jnp.where(visible, scores, -1e30)
    row_top = jnp.max(scores, axis=-1, keepdims=True)
    raw_weights = jnp.where(visible, jnp.exp(scores - row_top), 0.0)
    totals = jnp.sum(raw_weights, axis=-1)
    weights_low = raw_weights.astype(jnp.bfloat16).reshape(
        requests, half_rows, kv_dev, per_kv, pages_max, page_rows
    )
    weighted = jnp.einsum(
        "rukgpw,rpkwd->rukgd", weights_low, values_part, preferred_element_type=jnp.float32
    )
    attended = (
        (weighted / totals[..., None])
        .astype(jnp.bfloat16)
        .reshape(requests * half_rows, heads_dev * head_dim)
    )
    projected = lax.psum_scatter(
        jnp.dot(attended, out_weight, preferred_element_type=jnp.float32).astype(jnp.bfloat16),
        "tp",
        scatter_dimension=0,
        tiled=True,
    ).astype(jnp.float32)
    mid_state = residual.astype(jnp.float32) + projected
    routed_dev = tok_dev * TOPK // EXPERTS
    row_lists = []
    gate_lists = []
    for expert in range(EXP_WIN):
        names_it = expert_ids == expert
        chosen_rows = jnp.nonzero(jnp.any(names_it, axis=-1), size=routed_dev)[0].astype(jnp.int32)
        row_lists.append(chosen_rows)
        gate_lists.append(jnp.sum(jnp.where(names_it, expert_gates, 0.0), axis=-1)[chosen_rows])
    picked_rows = jnp.stack(row_lists, axis=1)
    picked_gates = jnp.stack(gate_lists, axis=1)
    selected = mid_state[picked_rows]
    inverse = lax.rsqrt(jnp.mean(selected * selected, axis=-1, keepdims=True) + 1e-05)
    normed = (selected * inverse * moe_gain).astype(jnp.bfloat16)
    exp_dec = w_gate.shape[0]
    width = normed.shape[2]
    by_expert = normed.reshape(routed_dev, dec_size, exp_dec, width)
    row_piece = lax.dynamic_index_in_dim(
        lax.all_gather(by_expert, ("tp", "dec"), axis=0, tiled=True), dec_index, 1, keepdims=False
    )
    gate_part = jnp.einsum("ned,efd->nef", row_piece, w_gate, preferred_element_type=jnp.float32)
    up_part = jnp.einsum("ned,efd->nef", row_piece, w_up, preferred_element_type=jnp.float32)
    hidden = (jax.nn.silu(gate_part) * up_part).astype(jnp.bfloat16)
    expert_part = lax.psum_scatter(
        jnp.einsum("nef,efd->ned", hidden, w_down, preferred_element_type=jnp.float32).astype(
            jnp.bfloat16
        ),
        "tp",
        scatter_dimension=0,
        tiled=True,
    ).astype(jnp.float32)
    expert_part = expert_part.reshape(dec_size, routed_dev, exp_dec, width)
    expert_out = (
        lax.all_to_all(
            expert_part.astype(jnp.bfloat16), "dec", split_axis=0, concat_axis=2, tiled=True
        )
        .astype(expert_part.dtype)
        .reshape(routed_dev, dec_size * exp_dec, width)
    )
    mixture = jnp.zeros_like(mid_state)
    for expert in range(EXP_WIN):
        mixture = mixture.at[picked_rows[:, expert]].add(
            expert_out[:, expert] * picked_gates[:, expert][:, None]
        )
    layer_out = (mid_state + mixture).astype(jnp.bfloat16)
    decode_pages = hand_over(kv_pool, page_target)
    return (layer_out, decode_pages)


def solution(mesh):
    return jax.shard_map(
        on_device,
        mesh=mesh,
        in_specs=(
            P(("rep", "tp", "dec"), None),
            P("rep", "dec", None, "tp"),
            P(("rep", "tp", "dec"), None, None, None),
            P("rep"),
            P("rep", None),
            P(("rep", "tp", "dec")),
            P("tp", None),
            P(),
            P(("rep", "tp", "dec"), None),
            P(("rep", "tp", "dec"), None),
            P("dec", "tp", None),
            P("dec", "tp", None),
            P("dec", "tp", None),
        ),
        out_specs=(P(("rep", "tp", "dec"), None), P(("rep", "tp", "dec"), None, None, None)),
        check_vma=False,
    )
```

profile of v0, /device:TPU:4, one launch (start us, length us, event | category | flops | bytes accessed | tf_op | source)
XLA Modules:
  0.0 915.2 jit_solution(17047965572777546698)
XLA Ops:
  7.2 1.4 broadcast_in_dim.77
  8.5 2.7 broadcast_in_dim.79
  11.2 13.1 %all-to-all-start = ((bf16[1,64,1,128,256]{4,3,2,0,1:T(8,128)(2,1)}), bf16[1,64,1,128,256]{4,3,2,0,1:T(8,128)(2,1)}, u32[]{:S(2)}, u32[]{:S(2)}) async-start(bf16[1,64,1,128,256]{4,3,2,0,1:T(8,128)(2,1)} %bitcast.171), calls=%async_computation | async-start | bytes 8388608 | tf_op jit(solution)/shard_map/all_to_all | solution.py:61
  24.5 0.1 reshape.483
  24.6 0.1 broadcast_add_fusion
  24.6 95.0 %all-to-all-done = bf16[1,64,1,128,256]{4,3,2,0,1:T(8,128)(2,1)} async-done(((bf16[1,64,1,128,256]{4,3,2,0,1:T(8,128)(2,1)}), bf16[1,64,1,128,256]{4,3,2,0,1:T(8,128)(2,1)}, u32[]{:S(2)}, u32[]{:S(2)}) %all-to-all-start) | async-done | bytes 4194336 | tf_op jit(solution)/shard_map/all_to_all | solution.py:61
  119.6 5.0 gather_fusion
  124.6 2.4 fusion.6
  127.0 1.3 fusion.7
  128.3 1.7 fusion.39
  130.1 3.2 convolution_convert_fusion
  133.3 0.1 copy.34
  133.5 0.1 fusion.60
  133.6 0.7 scatter_custom_fusion
  134.2 0.2 select_n.264
  134.4 0.1 copy.35
  134.5 0.1 fusion.61
  134.7 0.7 scatter_custom_fusion.1
  135.3 0.2 select_n.269
  135.5 0.6 convert_reduce_fusion
  136.1 0.7 fusion.69
  136.8 0.7 fusion.70
  137.5 0.1 copy.36
  137.6 0.1 reshape.491
  137.7 214.3 %reduce-scatter.3.cloned.1.call-done = bf16[16,4096]{1,0:T(8,128)(2,1)} async-done(((bf16[512,4096]{1,0:T(8,128)(2,1)}), bf16[16,4096]{1,0:T(8,128)(2,1)}) %reduce-scatter.3.cloned.1.call-update) | async-done | bytes 131088 | tf_op jit(solution)/shard_map/reduce_scatter | solution.py:93
  352.0 0.9 convert_add_fusion
  353.0 0.6 gather_fusion.1
  353.6 0.1 gather.16
  353.6 0.1 multiply_reduce_fusion
  353.8 0.1 reshape.557
  353.9 0.8 fusion.51
  354.7 0.2 reduce-scatter.5.cloned.1.call-start
  354.9 302.4 %all-gather.2.cloned.1.call-done = bf16[256,2,1,4096]{3,1,2,0:T(2,128)(2,1)} async-done(((bf16[4,2,1,4096]{3,1,2,0:T(2,128)(2,1)}), bf16[256,2,1,4096]{3,1,2,0:T(2,128)(2,1)}) %all-gather.2.cloned.1.call-update) | async-done | bytes 4194320 | tf_op jit(solution)/shard_map/all_gather | solution.py:117
  657.3 9.2 %constant_dynamic-slice_fusion = bf16[256,1,1,4096]{3,1,2,0:T(2,128)(2,1)} fusion(bf16[256,2,1,4096]{3,1,2,0:T(2,128)(2,1)} %all-gather.2.cloned.1.call-done, s32[]{:T(128)S(6)} %select_n.273), kind=kLoop, calls=%fused_computation.114 | loop fusion | bytes 4194308 | tf_op jit(solution)/shard_map/jit(dynamic_index_in_dim)/dynamic_slice | solution.py:116
  666.6 6.2 fusion.18
  672.8 10.8 %fusion = bf16[256,1,4096]{2,0,1:T(8,128)(2,1)} fusion(bf16[1,448,4096]{2,1,0:T(8,128)(2,1)} %param.25, bf16[1,448,4096]{2,1,0:T(8,128)(2,1)} %param.24, bf16[256,1,1,4096]{3,1,2,0:T(2,128)(2,1)} %constant_dynamic-slice_fusion, f32[256,1,448]{0,2,1:T(8,128)S(1)} %fusion.18), kind=kOutput, calls=%fused_computation.12 | convolution fusion | flops 1880784896 | bytes 11993088 | tf_op jit(solution)/shard_map/nef,efd->ned/dot_general | solution.py:123
  684.2 1.6 broadcast_select_fusion
  685.8 4.8 all-to-all-start.2
  690.7 206.7 %reduce-scatter.5.cloned.1.call-done = bf16[8,1,4096]{2,0,1:T(8,128)(2,1)} async-done(((bf16[256,1,4096]{2,0,1:T(8,128)(2,1)}), bf16[8,1,4096]{2,0,1:T(8,128)(2,1)}) %reduce-scatter.5.cloned.1.call-update) | async-done | bytes 65552 | tf_op jit(solution)/shard_map/reduce_scatter | solution.py:122
  897.3 1.5 convert_element_type.130
  898.8 3.3 all-to-all-start.1
  902.1 0.6 gather_fusion.2
  902.8 0.6 gather_fusion.3
  903.4 1.3 reduce_sum.74
  904.7 1.5 all-to-all-done.1
  906.2 0.9 scatter_custom_fusion.2
  907.1 0.9 scatter_custom_fusion.3
  908.0 0.7 convert_element_type.135
  (43 shorter events, 0.4 us)
Async XLA Ops:
  7.2 122.9 %copy-start = (bf16[128,4096]{1,0:T(8,128)(2,1)S(1)}, bf16[128,4096]{1,0:T(8,128)(2,1)}, u32[]{:S(2)}) copy-start(bf16[128,4096]{1,0:T(8,128)(2,1)} %param.19) | copy-start | bytes 3145732
  11.2 13.2 %copy-start.6 = (s32[4,16]{1,0:T(4,128)S(1)}, s32[4,16]{1,0:T(4,128)}, u32[]{:S(2)}) copy-start(s32[4,16]{1,0:T(4,128)} %param.17) | copy-start | bytes 772
  11.2 13.3 %copy-start.8 = (s32[4]{0:T(128)S(1)}, s32[4]{0:T(128)}, u32[]{:S(2)}) copy-start(s32[4]{0:T(128)} %param.16) | copy-start | bytes 52
  11.2 108.4 %all-to-all-start = ((bf16[1,64,1,128,256]{4,3,2,0,1:T(8,128)(2,1)}), bf16[1,64,1,128,256]{4,3,2,0,1:T(8,128)(2,1)}, u32[]{:S(2)}, u32[]{:S(2)}) async-start(bf16[1,64,1,128,256]{4,3,2,0,1:T(8,128)(2,1)} %bitcast.171), calls=%async_computation | async-start | bytes 8388608 | tf_op jit(solution)/shard_map/all_to_all | solution.py:61
  24.4 327.6 %reduce-scatter.3.cloned.1.call-start = ((), (), s32[]{:S(2)}) async-start(), calls=%async_computation.5 | async-start | bytes 4325376 | tf_op jit(solution)/shard_map/reduce_scatter | solution.py:93
  119.6 5.0 copy-start.9
  124.6 3.7 copy-start.1
  130.0 3.3 copy-start.5
  130.0 222.0 %copy-start.3 = (bf16[16,4096]{1,0:T(8,128)(2,1)S(1)}, bf16[16,4096]{1,0:T(8,128)(2,1)}, u32[]{:S(2)}) copy-start(bf16[16,4096]{1,0:T(8,128)(2,1)} %param.13) | copy-start | bytes 393220
  133.2 220.7 %copy-start.4 = (f32[4096]{0:T(1024)S(1)}, f32[4096]{0:T(1024)}, u32[]{:S(2)}) copy-start(f32[4096]{0:T(1024)} %param.20) | copy-start | bytes 49156
  133.2 524.1 %all-gather.2.cloned.1.call-start = ((), (), s32[]{:S(2)}) async-start(), calls=%async_computation.6 | async-start | bytes 4259840 | tf_op jit(solution)/shard_map/all_gather | solution.py:117
  354.7 542.6 %reduce-scatter.5.cloned.1.call-start = ((), (), s32[]{:S(2)}) async-start(), calls=%async_computation.7 | async-start | bytes 2162688 | tf_op jit(solution)/shard_map/reduce_scatter | solution.py:122
  672.8 11.5 %copy-start.2 = (bf16[1,8,128,256]{3,2,1,0:T(8,128)(2,1)S(1)}, bf16[1,8,128,256]{3,2,1,0:T(8,128)(2,1)}, u32[]{:S(2)}) copy-start(bf16[1,8,128,256]{3,2,1,0:T(8,128)(2,1)} %param.15) | copy-start | bytes 1572868
  683.5 7.1 copy-start.7
  685.8 213.0 %all-to-all-start.2 = ((bf16[4,1,8,128,256]{4,3,2,1,0:T(8,128)(2,1)}), bf16[4,1,8,128,256]{4,3,2,1,0:T(8,128)(2,1)S(1)}, u32[]{:S(2)}, u32[]{:S(2)}) async-start(bf16[4,1,8,128,256]{4,3,2,1,0:T(8,128)(2,1)} %broadcast_select_fusion), calls=%async_computation.4 | async-start | bytes 4194304 | tf_op jit(solution)/shard_map/all_to_all | solution.py:18
  898.8 7.4 all-to-all-start.1
Sparse Core Ops, SparseCore 0:
  133.4 218.5 reduce-scatter.2
  354.8 302.4 all-gather.1
  683.7 213.5 reduce-scatter.4
where the time goes:
time: 916 us; the launch traced here: 915 us
  waiting for transfers between devices  820 us (90%)
  matrix products  24.2 us (3%)
  local copies, waits for them, and re-layouts  22.3 us (2%)
  starting transfers between devices  21.5 us (2%)
  between operations  14.6 us (2%)
  other arithmetic  12.5 us (1%)
    all_gather x1, waiting for transfers between devices, on_device(): lax.all_gather(by_expert, ('tp', 'dec'), axis=0, tiled=True)  302 us
    reduce_scatter x1, waiting for transfers between devices, on_device(): lax.psum_scatter(jnp.dot(attended, out_weight, preferred_element_type=jnp...  214 us
    reduce_scatter x1, waiting for transfers between devices, on_device(): lax.psum_scatter(jnp.einsum('nef,efd->ned', hidden, w_down, preferred_ele...  207 us
    all_to_all x1, waiting for transfers between devices, on_device(): lax.all_to_all(outgoing, ('tp', 'dec'), split_axis=1, concat_axis=0, tile...  95 us
  transfers between devices with their start and end apart: 6, of which 5 were waited for; matrix products, arithmetic and copies ran while one was open for 1% of the time, Pallas kernels for 0%

commit v1 on v0

--- a/solution.py
+++ b/solution.py
@@ -114,7 +114,18 @@
     width = normed.shape[2]
     by_expert = normed.reshape(routed_dev, dec_size, exp_dec, width)
     row_piece = lax.dynamic_index_in_dim(
-        lax.all_gather(by_expert, ("tp", "dec"), axis=0, tiled=True), dec_index, 1, keepdims=False
+        jnp.concatenate(
+            lax.all_to_all(
+                jnp.stack([by_expert for _ in range(lax.axis_size(("tp", "dec")))]),
+                ("tp", "dec"),
+                0,
+                0,
+            ),
+            axis=0,
+        ),
+        dec_index,
+        1,
+        keepdims=False,
     )
     gate_part = jnp.einsum("ned,efd->nef", row_piece, w_gate, preferred_element_type=jnp.float32)
     up_part = jnp.einsum("ned,efd->nef", row_piece, w_up, preferred_element_type=jnp.float32)

time: 916 us -> 717 us (0.78)
  waiting for transfers between devices: 820 us -> 608 us
    all_gather x1 -> x0, waiting for transfers between devices: 302 us -> none  [on_device(): lax.all_gather(by_expert, ('tp', 'dec'), axis=0, tiled=True)]
    all_to_all x0 -> x1, waiting for transfers between devices: none -> 90 us  [on_device(): lax.all_to_all(jnp.stack([by_expert for _ in range(lax.axis_size(('tp', '...]
where the time goes in v1:
time: 717 us; the launch traced here: 716 us
  waiting for transfers between devices  608 us (85%)
  starting transfers between devices  29.7 us (4%)
  local copies, waits for them, and re-layouts  28.2 us (4%)
  matrix products  23.1 us (3%)
  between operations  15 us (2%)
  other arithmetic  11.9 us (2%)
    reduce_scatter x1, waiting for transfers between devices, on_device(): lax.psum_scatter(jnp.dot(attended, out_weight, preferred_element_type=jnp...  214 us
    reduce_scatter x1, waiting for transfers between devices, on_device(): lax.psum_scatter(jnp.einsum('nef,efd->ned', hidden, w_down, preferred_ele...  207 us
    all_to_all x1, waiting for transfers between devices, on_device(): lax.all_to_all(outgoing, ('tp', 'dec'), split_axis=1, concat_axis=0, tile...  95 us
    all_to_all x1, waiting for transfers between devices, on_device(): lax.all_to_all(jnp.stack([by_expert for _ in range(lax.axis_size(('tp', '...  90 us
  transfers between devices with their start and end apart: 6, of which 5 were waited for; matrix products, arithmetic and copies ran while one was open for 1% of the time, Pallas kernels for 0%

profile of v1, /device:TPU:4, one launch (start us, length us, event | category | flops | bytes accessed | tf_op | source)
XLA Modules:
  0.0 715.9 jit_solution(16186729135136765823)
XLA Ops:
  7.2 1.4 broadcast_in_dim.77
  8.5 2.7 broadcast_in_dim.79
  11.2 13.1 %all-to-all-start = ((bf16[1,64,1,128,256]{4,3,2,0,1:T(8,128)(2,1)}), bf16[1,64,1,128,256]{4,3,2,0,1:T(8,128)(2,1)}, u32[]{:S(2)}, u32[]{:S(2)}) async-start(bf16[1,64,1,128,256]{4,3,2,0,1:T(8,128)(2,1)} %bitcast.177), calls=%async_computation | async-start | bytes 8388608 | tf_op jit(solution)/shard_map/all_to_all | solution.py:61
  24.5 0.1 reshape.481
  24.6 95.0 %all-to-all-done = bf16[1,64,1,128,256]{4,3,2,0,1:T(8,128)(2,1)} async-done(((bf16[1,64,1,128,256]{4,3,2,0,1:T(8,128)(2,1)}), bf16[1,64,1,128,256]{4,3,2,0,1:T(8,128)(2,1)}, u32[]{:S(2)}, u32[]{:S(2)}) %all-to-all-start) | async-done | bytes 4194336 | tf_op jit(solution)/shard_map/all_to_all | solution.py:61
  119.6 5.0 gather_fusion
  124.6 2.4 fusion.6
  127.0 1.3 fusion.7
  128.3 1.7 fusion.51
  130.1 3.2 convolution_convert_fusion
  133.3 0.1 copy.30
  133.4 0.1 fusion.74
  133.5 0.7 scatter_custom_fusion
  134.2 0.2 select_n.264
  134.5 0.1 fusion.75
  134.6 0.7 scatter_custom_fusion.1
  135.3 0.2 select_n.269
  135.5 0.6 convert_reduce_fusion
  136.1 0.7 fusion.83
  136.8 0.7 fusion.84
  137.4 0.1 copy.32
  137.5 0.1 reshape.489
  137.6 214.4 %reduce-scatter.3.cloned.1.call-done = bf16[16,4096]{1,0:T(8,128)(2,1)} async-done(((bf16[512,4096]{1,0:T(8,128)(2,1)}), bf16[16,4096]{1,0:T(8,128)(2,1)}) %reduce-scatter.3.cloned.1.call-update) | async-done | bytes 131088 | tf_op jit(solution)/shard_map/reduce_scatter | solution.py:93
  352.0 0.9 convert_add_fusion
  352.9 0.6 gather_fusion.1
  353.5 0.1 reshape.488
  353.6 0.1 multiply_reduce_fusion
  353.8 0.1 multiply_convert_fusion
  353.9 6.2 stack.17
  360.1 8.2 %all-to-all-start.1 = ((bf16[64,4,2,1,4096]{4,2,1,3,0:T(2,128)(2,1)}), bf16[64,4,2,1,4096]{4,2,1,3,0:T(2,128)(2,1)}, u32[]{:S(2)}, u32[]{:S(2)}) async-start(bf16[64,4,2,1,4096]{4,2,1,3,0:T(2,128)(2,1)} %stack.17), calls=%async_computation.2 | async-start | bytes 8388608 | tf_op jit(solution)/shard_map/all_to_all | solution.py:118
  368.3 0.2 reduce-scatter.5.cloned.1.call-start
  368.6 90.0 %all-to-all-done.1 = bf16[64,4,2,1,4096]{4,2,1,3,0:T(2,128)(2,1)} async-done(((bf16[64,4,2,1,4096]{4,2,1,3,0:T(2,128)(2,1)}), bf16[64,4,2,1,4096]{4,2,1,3,0:T(2,128)(2,1)}, u32[]{:S(2)}, u32[]{:S(2)}) %all-to-all-start.1) | async-done | bytes 4194336 | tf_op jit(solution)/shard_map/all_to_all | solution.py:118
  458.6 7.0 constant_dynamic-slice_fusion
  465.6 1.9 copy-done.2
  467.5 5.1 fusion.20
  472.6 10.8 %fusion = bf16[256,1,4096]{2,0,1:T(8,128)(2,1)} fusion(bf16[1,448,4096]{2,1,0:T(8,128)(2,1)} %param.25, bf16[1,448,4096]{2,1,0:T(8,128)(2,1)} %param.24, bf16[256,1,1,4096]{3,1,0,2:T(2,128)(2,1)} %copy-done.2, f32[256,1,448]{0,2,1:T(8,128)S(1)} %fusion.20), kind=kOutput, calls=%fused_computation.12 | convolution fusion | flops 1880784896 | bytes 11993088 | tf_op jit(solution)/shard_map/nef,efd->ned/dot_general | solution.py:134
  484.1 1.6 broadcast_select_fusion
  485.7 4.8 all-to-all-start.3
  490.5 207.2 %reduce-scatter.5.cloned.1.call-done = bf16[8,1,4096]{2,0,1:T(8,128)(2,1)} async-done(((bf16[256,1,4096]{2,0,1:T(8,128)(2,1)}), bf16[8,1,4096]{2,0,1:T(8,128)(2,1)}) %reduce-scatter.5.cloned.1.call-update) | async-done | bytes 65552 | tf_op jit(solution)/shard_map/reduce_scatter | solution.py:133
  697.7 1.5 convert_element_type.128
  699.2 3.3 all-to-all-start.2
  702.5 0.6 gather_fusion.2
  703.1 0.6 gather_fusion.3
  703.8 1.3 reduce_sum.74
  705.0 1.5 all-to-all-done.2
  706.6 0.9 scatter_custom_fusion.2
  707.5 0.9 scatter_custom_fusion.3
  708.4 0.7 convert_element_type.133
  (44 shorter events, 0.5 us)
Async XLA Ops:
  7.2 122.9 %copy-start = (bf16[128,4096]{1,0:T(8,128)(2,1)S(1)}, bf16[128,4096]{1,0:T(8,128)(2,1)}, u32[]{:S(2)}) copy-start(bf16[128,4096]{1,0:T(8,128)(2,1)} %param.19) | copy-start | bytes 3145732
  11.2 13.2 %copy-start.7 = (s32[4,16]{1,0:T(4,128)S(1)}, s32[4,16]{1,0:T(4,128)}, u32[]{:S(2)}) copy-start(s32[4,16]{1,0:T(4,128)} %param.17) | copy-start | bytes 772
  11.2 13.3 %copy-start.9 = (s32[4]{0:T(128)S(1)}, s32[4]{0:T(128)}, u32[]{:S(2)}) copy-start(s32[4]{0:T(128)} %param.16) | copy-start | bytes 52
  11.2 108.4 %all-to-all-start = ((bf16[1,64,1,128,256]{4,3,2,0,1:T(8,128)(2,1)}), bf16[1,64,1,128,256]{4,3,2,0,1:T(8,128)(2,1)}, u32[]{:S(2)}, u32[]{:S(2)}) async-start(bf16[1,64,1,128,256]{4,3,2,0,1:T(8,128)(2,1)} %bitcast.177), calls=%async_computation | async-start | bytes 8388608 | tf_op jit(solution)/shard_map/all_to_all | solution.py:61
  24.4 327.6 %reduce-scatter.3.cloned.1.call-start = ((), (), s32[]{:S(2)}) async-start(), calls=%async_computation.6 | async-start | bytes 4325376 | tf_op jit(solution)/shard_map/reduce_scatter | solution.py:93
  119.6 5.0 copy-start.10
  124.6 3.7 copy-start.1
  130.0 3.2 copy-start.6
  130.0 221.9 %copy-start.4 = (bf16[16,4096]{1,0:T(8,128)(2,1)S(1)}, bf16[16,4096]{1,0:T(8,128)(2,1)}, u32[]{:S(2)}) copy-start(bf16[16,4096]{1,0:T(8,128)(2,1)} %param.13) | copy-start | bytes 393220
  133.2 220.6 %copy-start.5 = (f32[4096]{0:T(1024)S(1)}, f32[4096]{0:T(1024)}, u32[]{:S(2)}) copy-start(f32[4096]{0:T(1024)} %param.20) | copy-start | bytes 49156
  360.1 98.4 %all-to-all-start.1 = ((bf16[64,4,2,1,4096]{4,2,1,3,0:T(2,128)(2,1)}), bf16[64,4,2,1,4096]{4,2,1,3,0:T(2,128)(2,1)}, u32[]{:S(2)}, u32[]{:S(2)}) async-start(bf16[64,4,2,1,4096]{4,2,1,3,0:T(2,128)(2,1)} %stack.17), calls=%async_computation.2 | async-start | bytes 8388608 | tf_op jit(solution)/shard_map/all_to_all | solution.py:118
  368.3 329.3 %reduce-scatter.5.cloned.1.call-start = ((), (), s32[]{:S(2)}) async-start(), calls=%async_computation.7 | async-start | bytes 2162688 | tf_op jit(solution)/shard_map/reduce_scatter | solution.py:133
  465.6 1.9 copy-start.2
  472.6 11.5 %copy-start.3 = (bf16[1,8,128,256]{3,2,1,0:T(8,128)(2,1)S(1)}, bf16[1,8,128,256]{3,2,1,0:T(8,128)(2,1)}, u32[]{:S(2)}) copy-start(bf16[1,8,128,256]{3,2,1,0:T(8,128)(2,1)} %param.15) | copy-start | bytes 1572868
  483.4 7.1 copy-start.8
  485.7 213.5 %all-to-all-start.3 = ((bf16[4,1,8,128,256]{4,3,2,1,0:T(8,128)(2,1)}), bf16[4,1,8,128,256]{4,3,2,1,0:T(8,128)(2,1)S(1)}, u32[]{:S(2)}, u32[]{:S(2)}) async-start(bf16[4,1,8,128,256]{4,3,2,1,0:T(8,128)(2,1)} %broadcast_select_fusion), calls=%async_computation.5 | async-start | bytes 4194304 | tf_op jit(solution)/shard_map/all_to_all | solution.py:18
  699.2 7.4 %all-to-all-start.2 = ((bf16[2,4,1,4096]{3,1,2,0:T(4,128)(2,1)}), bf16[2,4,1,4096]{3,1,2,0:T(4,128)(2,1)S(1)}, u32[]{:S(2)}, u32[]{:S(2)}) async-start(bf16[2,4,1,4096]{3,1,2,0:T(4,128)(2,1)} %bitcast.41), calls=%async_computation.4 | async-start | bytes 131072 | tf_op jit(solution)/shard_map/all_to_all | solution.py:143
Sparse Core Ops, SparseCore 0:
  133.4 218.5 reduce-scatter.2
  483.5 214.0 reduce-scatter.4
